TPU v7x, 32 devices: a whole 2x2x4 slice. The times are simulated.
32 devices in a mesh: occ: 8 (over y, x, core), vir: 4 (over z).
Axes of the slice: x: 2, y: 2, z: 4, core: 2. Of those that a mesh axis runs over, the one named last changes fastest.
Arguments:
- factors: bfloat16 [8, 1024, 2048], P('occ', 'vir'), may hold values from -0.047851562 to 0.047851562
- occupied_energy: float32 [8], replicated, may hold values from -1.5 to -0.5
- virtual_energy: float32 [1024], replicated, may hold values from 0.2 to 3
Outputs:
- dens_vv: float32 [1024, 1024], P(('occ', 'vir'))
- dens_oo: float32 [8, 8], replicated
All inputs are finite; a program needn't handle non-finite values.
Results may differ from a plain program's by a relative error of at most 0.0065.
Values may be sent and summed in bfloat16 or wider, within the bound.
No kernel may reach another device: no remote copies, remote signals or barrier semaphores. Data moves between devices by JAX's collectives and lax.ppermute only.
A program may use at most 64 MiB of HBM per device.

v0:
```python
import jax
import jax.numpy as jnp
from jax import lax
from jax.sharding import PartitionSpec as P


def from_behind(shard, axis, by):
    length = lax.axis_size(axis)
    return lax.ppermute(shard, axis, [(i, (i + by) % length) for i in range(length)])


def on_device(factors, occupied_energy, virtual_energy):
    orbitals = factors.shape[0]
    vblock = factors.shape[1]
    nvir_all = virtual_energy.shape[0]
    nbatch_all = occupied_energy.shape[0]
    occ_count = lax.axis_size("occ")
    vir_count = lax.axis_size("vir")
    partners = occ_count // 4
    occ_pos = lax.axis_index("occ")
    vir_pos = lax.axis_index("vir")
    highest = lax.Precision.HIGHEST
    whole = lax.all_gather(factors, "vir", axis=1, tiled=True)

    def tiles(block):
        return jnp.einsum(
            "sjyp,ixp->isjyx", block, whole, preferred_element_type=jnp.float32
        ).astype(jnp.bfloat16)

    stack = jnp.zeros((orbitals, partners, orbitals, vblock, nvir_all), jnp.bfloat16)
    stack = lax.dynamic_update_slice_in_dim(stack, tiles(factors[None]), 0, 1)

    def advance(position, carry):
        current, filled = carry
        current = from_behind(current, "occ", -1)
        filled = lax.dynamic_update_slice_in_dim(filled, tiles(current[None]), position, 1)
        return (current, filled)

    _, stack = lax.fori_loop(1, partners, advance, (factors, stack))
    sending = stack.reshape(orbitals, partners, orbitals, vblock, vir_count, nvir_all // vir_count)
    received = lax.all_to_all(sending, "vir", split_axis=4, concat_axis=4, tiled=True)
    coulomb = received.transpose(0, 1, 2, 5, 4, 3).reshape(
        orbitals, partners, orbitals, vblock, nvir_all
    )
    batch_ids = (occ_pos + jnp.arange(partners, dtype=jnp.int32)) % occ_count
    global_ids = (
        batch_ids[:, None] * orbitals + jnp.arange(orbitals, dtype=jnp.int32)[None, :]
    ).reshape(-1)
    onehot = (global_ids[:, None] == jnp.arange(nbatch_all, dtype=jnp.int32)[None, :]).astype(
        jnp.float32
    )
    partner_energy = jnp.dot(onehot, occupied_energy, precision=highest).reshape(partners, orbitals)
    own_energy = lax.dynamic_slice_in_dim(occupied_energy, occ_pos * orbitals, orbitals)
    local_vir = lax.dynamic_slice_in_dim(virtual_energy, vir_pos * vblock, vblock)
    denom = (
        own_energy[:, None, None, None, None]
        + partner_energy[None, :, :, None, None]
        - local_vir[:, None]
        - virtual_energy
    )
    amps = (coulomb.astype(jnp.float32) / denom).astype(jnp.bfloat16)
    tilde = ((2.0 * coulomb.astype(jnp.float32) - stack.astype(jnp.float32)) / denom).astype(
        jnp.bfloat16
    )
    flat_amps = amps.reshape(-1, nvir_all)
    flat_tilde = tilde.reshape(-1, nvir_all)
    partial_rows = lax.psum_scatter(
        lax.dot_general(
            flat_amps, flat_tilde, (((0,), (0,)), ((), ())), preferred_element_type=jnp.float32
        ).astype(jnp.bfloat16),
        "occ",
        scatter_dimension=0,
        tiled=True,
    ).astype(jnp.float32)
    dens_vv = lax.psum_scatter(partial_rows, "vir", scatter_dimension=0, tiled=True)
    amps_rows = amps.reshape(orbitals, partners * orbitals, -1)
    tilde_rows = tilde.reshape(orbitals, partners * orbitals, -1)
    gram = -lax.dot_general(
        amps_rows, tilde_rows, (((2,), (2,)), ((0,), (0,))), preferred_element_type=jnp.float32
    )
    gram_sum = jnp.sum(gram, axis=0)
    placed = jnp.dot(onehot.T, jnp.dot(gram_sum, onehot, precision=highest), precision=highest)
    dens_oo = lax.psum(placed, ("occ", "vir"))
    return (dens_vv, dens_oo)


def solution(mesh):
    return jax.shard_map(
        on_device,
        mesh=mesh,
        in_specs=(P("occ", "vir", None), P(), P()),
        out_specs=(P(("occ", "vir"), None), P()),
        check_vma=False,
    )
```

profile of v0, /device:TPU:0, one launch (start us, length us, event | category | flops | bytes accessed | tf_op | source)
XLA Modules:
  0.0 227.3 jit_solution(8085726508122237578)
XLA Ops:
  7.2 0.0 all-gather.2.cloned.1.call-start
  7.2 0.7 all-gather.2.cloned.1.call-update
  7.9 3.4 %collective-permute-start = (bf16[1,256,2048]{2,1,0:T(8,128)(2,1)}, bf16[1,256,2048]{2,1,0:T(8,128)(2,1)S(1)}, u32[]{:S(2)}, u32[]{:S(2)}) collective-permute-start(bf16[1,256,2048]{2,1,0:T(8,128)(2,1)} %param.3), channel_id=1, source_target_pairs={{0,28},{4,0},{8,4},{12,8},{16,12},{20,16},{24,20},{28,24},{1,29},{... | collective-permute-start | bytes 3145736 | tf_op jit(solution)/shard_map/while/body/eval_jaxpr/ppermute | solution.py:9
  11.3 81.7 %all-gather.2.cloned.1.call-done = bf16[1,1024,2048]{2,1,0:T(8,128)(2,1)} async-done(((bf16[1,256,2048]{2,1,0:T(8,128)(2,1)}), bf16[1,1024,2048]{2,1,0:T(8,128)(2,1)}) %all-gather.2.cloned.1.call-update) | async-done | bytes 4194320 | tf_op jit(solution)/shard_map/all_gather | solution.py:23
  93.0 0.0 copy-start.3
  93.0 3.9 %fusion.7 = bf16[1024,256]{1,0:T(8,128)(2,1)S(1)} fusion(bf16[1,1024,2048]{2,1,0:T(8,128)(2,1)} %all-gather.2.cloned.1.call-done, bf16[1,256,2048]{2,1,0:T(8,128)(2,1)} %param.3), kind=kOutput, calls=%fused_computation.11 | convolution fusion | flops 1074003968 | bytes 5767168 | tf_op jit(solution)/shard_map/sjyp,ixp->isjyx/dot_general | solution.py:26
  97.0 0.0 copy-start
  97.0 0.0 collective-permute-done
  97.0 0.0 copy-done.3
  97.0 1.4 fusion.10
  98.4 0.0 copy-start.1
  98.4 0.0 copy-done
  98.4 0.1 pad_maximum_fusion
  98.5 0.0 copy-start.2
  98.5 0.0 copy-start.4
  98.5 1.3 copy.10
  99.8 0.0 copy-done.1
  99.8 3.5 %all-to-all-start = ((bf16[1,2,1,256,4,256]{5,3,2,1,0,4:T(8,128)(2,1)}), bf16[1,2,1,256,4,256]{5,3,2,1,0,4:T(8,128)(2,1)S(1)}, u32[]{:S(2)}, u32[]{:S(2)}) async-start(bf16[1,2,1,256,4,256]{5,3,2,1,0,4:T(8,128)(2,1)} %copy.10), calls=%async_computation | async-start | bytes 2097152 | tf_op jit(solution)/shard_map/all_to_all | solution.py:41
  103.3 0.0 reduce-scatter.3.cloned.1.call-start
  103.4 0.0 copy-done.2
  103.4 0.1 dynamic_slice.7
  103.5 0.0 copy-done.4
  103.5 0.6 dynamic_slice.6
  104.1 0.8 fusion.14
  104.9 0.1 broadcast_subtract_fusion
  105.0 24.2 %all-to-all-done = bf16[1,2,1,256,4,256]{5,3,2,1,0,4:T(8,128)(2,1)S(1)} async-done(((bf16[1,2,1,256,4,256]{5,3,2,1,0,4:T(8,128)(2,1)}), bf16[1,2,1,256,4,256]{5,3,2,1,0,4:T(8,128)(2,1)S(1)}, u32[]{:S(2)}, u32[]{:S(2)}) %all-to-all-start) | async-done | bytes 1048608 | tf_op jit(solution)/shard_map/all_to_all | solution.py:41
  129.2 1.9 fusion.5
  131.0 2.6 %bitcast_convert_fusion = bf16[1024,1024]{1,0:T(8,128)(2,1)} fusion(bf16[2,256,1024]{1,2,0:T(8,128)(2,1)S(1)} %bitcast.65, bf16[2,256,1024]{1,2,0:T(8,128)(2,1)S(1)} %bitcast.63), kind=kOutput, calls=%fused_computation | convolution fusion | flops 1074790400 | bytes 4194304 | tf_op jit(solution)/shard_map/dot_general | solution.py:68
  133.7 0.0 reduce-scatter.3.cloned.1.call-update
  133.7 0.0 reduce-scatter.5.cloned.1.call-start
  133.7 40.3 %reduce-scatter.3.cloned.1.call-done = bf16[128,1024]{1,0:T(8,128)(2,1)} async-done(((bf16[1024,1024]{1,0:T(8,128)(2,1)}), bf16[128,1024]{1,0:T(8,128)(2,1)}) %reduce-scatter.3.cloned.1.call-update) | async-done | bytes 262160 | tf_op jit(solution)/shard_map/reduce_scatter | solution.py:67
  174.0 1.8 convert_element_type.89
  175.8 0.0 reduce-scatter.5.cloned.1.call-update
  175.8 1.1 copy.15
  176.9 1.1 copy.16
  178.1 3.0 %fusion.13 = f32[2,2]{1,0:T(2,128)S(1)} fusion(bf16[2,256,4,256]{3,0,2,1:T(2,128)(2,1)S(1)} %copy.15, bf16[2,256,4,256]{3,0,2,1:T(2,128)(2,1)S(1)} %copy.16), kind=kOutput, calls=%fused_computation.14 | convolution fusion | flops 2097156 | bytes 2097168 | tf_op jit(solution)/shard_map/dot_general | solution.py:78
  181.1 0.2 fusion.18
  181.3 0.3 fusion.17
  181.5 39.2 %psum.7 = f32[8,8]{1,0:T(8,128)} all-reduce(f32[8,8]{1,0:T(8,128)S(1)} %fusion.17), channel_id=1, replica_groups=mesh['occ'=8,'vir'=4] {'occ','vir'}, use_global_device_ids=true, to_apply=%region_2.3 | all-reduce | flops 64 | bytes 512 | tf_op jit(solution)/shard_map/psum | solution.py:83
  220.8 0.0 reduce-scatter.5.cloned.1.call-done
  (2 shorter events, 0.0 us)
Async XLA Ops:
  7.2 85.9 %all-gather.2.cloned.1.call-start = ((), (), s32[]{:S(2)}) async-start(), calls=%async_computation.3 | async-start | bytes 5242880 | tf_op jit(solution)/shard_map/all_gather | solution.py:23
  7.9 89.1 %collective-permute-start = (bf16[1,256,2048]{2,1,0:T(8,128)(2,1)}, bf16[1,256,2048]{2,1,0:T(8,128)(2,1)S(1)}, u32[]{:S(2)}, u32[]{:S(2)}) collective-permute-start(bf16[1,256,2048]{2,1,0:T(8,128)(2,1)} %param.3), channel_id=1, source_target_pairs={{0,28},{4,0},{8,4},{12,8},{16,12},{20,16},{24,20},{28,24},{1,29},{... | collective-permute-start | bytes 3145736 | tf_op jit(solution)/shard_map/while/body/eval_jaxpr/ppermute | solution.py:9
  93.0 4.0 %copy-start.3 = (bf16[1,1024,2048]{2,1,0:T(8,128)(2,1)S(1)}, bf16[1,1024,2048]{2,1,0:T(8,128)(2,1)}, u32[]{:S(2)}) copy-start(bf16[1,1024,2048]{2,1,0:T(8,128)(2,1)} %all-gather.2.cloned.1.call-done) | copy-start | bytes 12582916
  97.0 1.4 copy-start
  98.4 1.4 copy-start.1
  98.5 4.9 %copy-start.2 = (f32[1024]{0:T(1024)S(1)}, f32[1024]{0:T(1024)}, u32[]{:S(2)}) copy-start(f32[1024]{0:T(1024)} %param.5) | copy-start | bytes 12292
  98.5 5.0 %copy-start.4 = (f32[8]{0:T(128)S(1)}, f32[8]{0:T(128)}, u32[]{:S(2)}) copy-start(f32[8]{0:T(128)} %param.4) | copy-start | bytes 100
  99.8 29.4 %all-to-all-start = ((bf16[1,2,1,256,4,256]{5,3,2,1,0,4:T(8,128)(2,1)}), bf16[1,2,1,256,4,256]{5,3,2,1,0,4:T(8,128)(2,1)S(1)}, u32[]{:S(2)}, u32[]{:S(2)}) async-start(bf16[1,2,1,256,4,256]{5,3,2,1,0,4:T(8,128)(2,1)} %copy.10), calls=%async_computation | async-start | bytes 2097152 | tf_op jit(solution)/shard_map/all_to_all | solution.py:41
  103.3 70.7 %reduce-scatter.3.cloned.1.call-start = ((), (), s32[]{:S(2)}) async-start(), calls=%async_computation.4 | async-start | bytes 2359296 | tf_op jit(solution)/shard_map/reduce_scatter | solution.py:67
  133.7 87.1 %reduce-scatter.5.cloned.1.call-start = ((), (), s32[]{:S(2)}) async-start(), calls=%async_computation.5 | async-start | bytes 655360 | tf_op jit(solution)/shard_map/reduce_scatter | solution.py:75
Sparse Core Ops, SparseCore 0:
  9.5 83.4 all-gather.1
  133.8 40.1 reduce-scatter.2
  176.9 21.8 reduce-scatter.4
where the time goes:
time: 228 us; the launch traced here: 227 us
  waiting for transfers between devices  147 us (64%)
  blocking collectives  39.2 us (17%)
  between operations  13.9 us (6%)
  matrix products  12.2 us (5%)
  starting transfers between devices  7.05 us (3%)
  local copies, waits for them, and re-layouts  4.21 us (2%)
  other arithmetic  3.84 us (2%)
    all_gather x1, waiting for transfers between devices, on_device(): whole = lax.all_gather(factors, 'vir', axis=1, tiled=True)  81.7 us
    reduce_scatter x1, waiting for transfers between devices, on_device(): lax.psum_scatter(lax.dot_general(flat_amps, flat_tilde, (((0,), (0,)), ((...  40.3 us
    psum x1, blocking collectives, on_device(): dens_oo = lax.psum(placed, ('occ', 'vir'))  39.2 us
    all_to_all x1, waiting for transfers between devices, on_device(): lax.all_to_all(sending, 'vir', split_axis=4, concat_axis=4, tiled=True)  24.2 us
    dot_general x2, matrix products, tiles(): jnp.einsum('sjyp,ixp->isjyx', block, whole, preferred_element_type=jnp.fl...  5.27 us
  transfers between devices with their start and end apart: 5, of which 3 were waited for; matrix products, arithmetic and copies ran while one was open for 5% of the time, Pallas kernels for 0%

commit v1 on v0

--- a/solution.py
+++ b/solution.py
@@ -80,7 +80,8 @@
     )
     gram_sum = jnp.sum(gram, axis=0)
     placed = jnp.dot(onehot.T, jnp.dot(gram_sum, onehot, precision=highest), precision=highest)
-    dens_oo = lax.psum(placed, ("occ", "vir"))
+    h_now = lax.all_gather(placed, axis_name=("occ", "vir"))
+    dens_oo = jnp.sum(h_now, axis=0)
     return (dens_vv, dens_oo)
 
 

time: 228 us -> 257 us (1.13)
  blocking collectives: 39.2 us -> 68.1 us
    all_gather x0 -> x1, blocking collectives: none -> 68.1 us  [on_device(): h_now = lax.all_gather(placed, axis_name=('occ', 'vir'))]
    psum x1 -> x0, blocking collectives: 39.2 us -> none  [on_device(): dens_oo = lax.psum(placed, ('occ', 'vir'))]
where the time goes in v1:
time: 257 us
  waiting for transfers between devices  147 us (57%)
  blocking collectives  68.1 us (26%)
  between operations  13.9 us (5%)
  matrix products  12.2 us (5%)
  starting transfers between devices  7.05 us (3%)
  other arithmetic  4.47 us (2%)
  local copies, waits for them, and re-layouts  4.21 us (2%)
    all_gather x1, waiting for transfers between devices, on_device(): whole = lax.all_gather(factors, 'vir', axis=1, tiled=True)  81.7 us
    all_gather x1, blocking collectives, on_device(): h_now = lax.all_gather(placed, axis_name=('occ', 'vir'))  68.1 us
    reduce_scatter x1, waiting for transfers between devices, on_device(): lax.psum_scatter(lax.dot_general(flat_amps, flat_tilde, (((0,), (0,)), ((...  40.3 us
    all_to_all x1, waiting for transfers between devices, on_device(): lax.all_to_all(sending, 'vir', split_axis=4, concat_axis=4, tiled=True)  24.2 us
    dot_general x2, matrix products, tiles(): jnp.einsum('sjyp,ixp->isjyx', block, whole, preferred_element_type=jnp.fl...  5.27 us
  transfers between devices with their start and end apart: 5, of which 3 were waited for; matrix products, arithmetic and copies ran while one was open for 5% of the time, Pallas kernels for 0%

profile of v1, /device:TPU:0, one launch (start us, length us, event | category | flops | bytes accessed | tf_op | source)
XLA Modules:
  0.0 256.8 jit_solution(14425997450792401202)
XLA Ops:
  7.2 0.0 all-gather.3.cloned.1.call-start
  7.2 0.7 all-gather.3.cloned.1.call-update
  7.9 3.4 %collective-permute-start = (bf16[1,256,2048]{2,1,0:T(8,128)(2,1)}, bf16[1,256,2048]{2,1,0:T(8,128)(2,1)S(1)}, u32[]{:S(2)}, u32[]{:S(2)}) collective-permute-start(bf16[1,256,2048]{2,1,0:T(8,128)(2,1)} %param.3), channel_id=1, source_target_pairs={{0,28},{4,0},{8,4},{12,8},{16,12},{20,16},{24,20},{28,24},{1,29},{... | collective-permute-start | bytes 3145736 | tf_op jit(solution)/shard_map/while/body/eval_jaxpr/ppermute | solution.py:9
  11.3 81.7 %all-gather.3.cloned.1.call-done = bf16[1,1024,2048]{2,1,0:T(8,128)(2,1)} async-done(((bf16[1,256,2048]{2,1,0:T(8,128)(2,1)}), bf16[1,1024,2048]{2,1,0:T(8,128)(2,1)}) %all-gather.3.cloned.1.call-update) | async-done | bytes 4194320 | tf_op jit(solution)/shard_map/all_gather | solution.py:23
  93.0 0.0 copy-start.3
  93.0 3.9 %fusion.7 = bf16[1024,256]{1,0:T(8,128)(2,1)S(1)} fusion(bf16[1,1024,2048]{2,1,0:T(8,128)(2,1)} %all-gather.3.cloned.1.call-done, bf16[1,256,2048]{2,1,0:T(8,128)(2,1)} %param.3), kind=kOutput, calls=%fused_computation.11 | convolution fusion | flops 1074003968 | bytes 5767168 | tf_op jit(solution)/shard_map/sjyp,ixp->isjyx/dot_general | solution.py:26
  97.0 0.0 copy-start
  97.0 0.0 collective-permute-done
  97.0 0.0 copy-done.3
  97.0 1.4 fusion.10
  98.4 0.0 copy-start.1
  98.4 0.0 copy-done
  98.4 0.1 pad_maximum_fusion
  98.5 0.0 copy-start.2
  98.5 0.0 copy-start.4
  98.5 1.3 copy.10
  99.8 0.0 copy-done.1
  99.8 3.5 %all-to-all-start = ((bf16[1,2,1,256,4,256]{5,3,2,1,0,4:T(8,128)(2,1)}), bf16[1,2,1,256,4,256]{5,3,2,1,0,4:T(8,128)(2,1)S(1)}, u32[]{:S(2)}, u32[]{:S(2)}) async-start(bf16[1,2,1,256,4,256]{5,3,2,1,0,4:T(8,128)(2,1)} %copy.10), calls=%async_computation | async-start | bytes 2097152 | tf_op jit(solution)/shard_map/all_to_all | solution.py:41
  103.3 0.0 reduce-scatter.3.cloned.1.call-start
  103.4 0.0 copy-done.2
  103.4 0.1 dynamic_slice.7
  103.5 0.0 copy-done.4
  103.5 0.6 dynamic_slice.6
  104.1 0.8 fusion.14
  104.9 0.1 broadcast_subtract_fusion
  105.0 24.2 %all-to-all-done = bf16[1,2,1,256,4,256]{5,3,2,1,0,4:T(8,128)(2,1)S(1)} async-done(((bf16[1,2,1,256,4,256]{5,3,2,1,0,4:T(8,128)(2,1)}), bf16[1,2,1,256,4,256]{5,3,2,1,0,4:T(8,128)(2,1)S(1)}, u32[]{:S(2)}, u32[]{:S(2)}) %all-to-all-start) | async-done | bytes 1048608 | tf_op jit(solution)/shard_map/all_to_all | solution.py:41
  129.2 1.9 fusion.5
  131.0 2.6 %bitcast_convert_fusion = bf16[1024,1024]{1,0:T(8,128)(2,1)} fusion(bf16[2,256,1024]{1,2,0:T(8,128)(2,1)S(1)} %bitcast.67, bf16[2,256,1024]{1,2,0:T(8,128)(2,1)S(1)} %bitcast.65), kind=kOutput, calls=%fused_computation | convolution fusion | flops 1074790400 | bytes 4194304 | tf_op jit(solution)/shard_map/dot_general | solution.py:68
  133.7 0.0 reduce-scatter.3.cloned.1.call-update
  133.7 0.0 reduce-scatter.5.cloned.1.call-start
  133.7 40.3 %reduce-scatter.3.cloned.1.call-done = bf16[128,1024]{1,0:T(8,128)(2,1)} async-done(((bf16[1024,1024]{1,0:T(8,128)(2,1)}), bf16[128,1024]{1,0:T(8,128)(2,1)}) %reduce-scatter.3.cloned.1.call-update) | async-done | bytes 262160 | tf_op jit(solution)/shard_map/reduce_scatter | solution.py:67
  174.0 1.8 convert_element_type.89
  175.8 0.0 reduce-scatter.5.cloned.1.call-update
  175.8 1.1 copy.15
  176.9 1.1 copy.16
  178.1 3.0 %fusion.13 = f32[2,2]{1,0:T(2,128)S(1)} fusion(bf16[2,256,4,256]{3,0,2,1:T(2,128)(2,1)S(1)} %copy.15, bf16[2,256,4,256]{3,0,2,1:T(2,128)(2,1)S(1)} %copy.16), kind=kOutput, calls=%fused_computation.14 | convolution fusion | flops 2097156 | bytes 2097168 | tf_op jit(solution)/shard_map/dot_general | solution.py:78
  181.1 0.2 fusion.18
  181.3 0.3 fusion.17
  181.5 68.1 %all-gather = f32[256,8]{1,0:T(8,128)S(1)} all-gather(f32[8,8]{1,0:T(8,128)S(1)} %fusion.17), channel_id=2, replica_groups=mesh['occ'=8,'vir'=4] {'occ','vir'}, dimensions={0}, use_global_device_ids=true | all-gather | bytes 8448 | tf_op jit(solution)/shard_map/all_gather | solution.py:83
  249.6 0.6 bitcast_reduce_fusion
  250.2 0.0 reduce-scatter.5.cloned.1.call-done
  (2 shorter events, 0.0 us)
Async XLA Ops:
  7.2 85.9 %all-gather.3.cloned.1.call-start = ((), (), s32[]{:S(2)}) async-start(), calls=%async_computation.3 | async-start | bytes 5242880 | tf_op jit(solution)/shard_map/all_gather | solution.py:23
  7.9 89.1 %collective-permute-start = (bf16[1,256,2048]{2,1,0:T(8,128)(2,1)}, bf16[1,256,2048]{2,1,0:T(8,128)(2,1)S(1)}, u32[]{:S(2)}, u32[]{:S(2)}) collective-permute-start(bf16[1,256,2048]{2,1,0:T(8,128)(2,1)} %param.3), channel_id=1, source_target_pairs={{0,28},{4,0},{8,4},{12,8},{16,12},{20,16},{24,20},{28,24},{1,29},{... | collective-permute-start | bytes 3145736 | tf_op jit(solution)/shard_map/while/body/eval_jaxpr/ppermute | solution.py:9
  93.0 4.0 %copy-start.3 = (bf16[1,1024,2048]{2,1,0:T(8,128)(2,1)S(1)}, bf16[1,1024,2048]{2,1,0:T(8,128)(2,1)}, u32[]{:S(2)}) copy-start(bf16[1,1024,2048]{2,1,0:T(8,128)(2,1)} %all-gather.3.cloned.1.call-done) | copy-start | bytes 12582916
  97.0 1.4 copy-start
  98.4 1.4 copy-start.1
  98.5 4.9 %copy-start.2 = (f32[1024]{0:T(1024)S(1)}, f32[1024]{0:T(1024)}, u32[]{:S(2)}) copy-start(f32[1024]{0:T(1024)} %param.5) | copy-start | bytes 12292
  98.5 5.0 %copy-start.4 = (f32[8]{0:T(128)S(1)}, f32[8]{0:T(128)}, u32[]{:S(2)}) copy-start(f32[8]{0:T(128)} %param.4) | copy-start | bytes 100
  99.8 29.4 %all-to-all-start = ((bf16[1,2,1,256,4,256]{5,3,2,1,0,4:T(8,128)(2,1)}), bf16[1,2,1,256,4,256]{5,3,2,1,0,4:T(8,128)(2,1)S(1)}, u32[]{:S(2)}, u32[]{:S(2)}) async-start(bf16[1,2,1,256,4,256]{5,3,2,1,0,4:T(8,128)(2,1)} %copy.10), calls=%async_computation | async-start | bytes 2097152 | tf_op jit(solution)/shard_map/all_to_all | solution.py:41
  103.3 70.7 %reduce-scatter.3.cloned.1.call-start = ((), (), s32[]{:S(2)}) async-start(), calls=%async_computation.4 | async-start | bytes 2359296 | tf_op jit(solution)/shard_map/reduce_scatter | solution.py:67
  133.7 116.6 %reduce-scatter.5.cloned.1.call-start = ((), (), s32[]{:S(2)}) async-start(), calls=%async_computation.5 | async-start | bytes 655360 | tf_op jit(solution)/shard_map/reduce_scatter | solution.py:75
Sparse Core Ops, SparseCore 0:
  9.5 83.4 all-gather.2
  133.8 40.1 reduce-scatter.2
  176.9 22.0 reduce-scatter.4
